TPU v7x, 32 devices: a whole 2x2x4 slice. The times are simulated.
32 devices in a mesh: clip: 2 (over core), tm: 16 (over z, y, x).
Axes of the slice: x: 2, y: 2, z: 4, core: 2. Of those that a mesh axis runs over, the one named last changes fastest.
Arguments:
- clip_frames: bfloat16 [2, 32, 64, 64, 128], P('clip', 'tm'), may hold values from -6 to 6
- spatial_weight: bfloat16 [3, 3, 128, 256], replicated, may hold values from -0.1875 to 0.1875
- norm_gain: float32 [256], replicated, may hold values from 0.5 to 1.5
- norm_bias: float32 [256], replicated, may hold values from -3 to 3
- temporal_weight: bfloat16 [3, 256, 256], replicated, may hold values from -0.21875 to 0.21875
- cotangent: bfloat16 [2, 32, 32, 32, 256], P('clip', 'tm'), may hold values from -0.0234375 to 0.0234375
Outputs:
- mixed: bfloat16 [2, 32, 32, 32, 256], P('clip', 'tm')
- spatial_grad: float32 [3, 3, 128, 256], replicated
- gain_grad: float32 [256], replicated
- bias_grad: float32 [256], replicated
- temporal_grad: float32 [3, 256, 256], replicated
All inputs are finite; a program needn't handle non-finite values.
Results may differ from a plain program's by a relative error of at most 0.0085.
Values may be sent and summed in bfloat16 or wider, within the bound.
A program may use at most 64 MiB of HBM per device.

v0:
```python
import jax
import jax.numpy as jnp
from jax import lax
from jax.sharding import PartitionSpec as P

GROUPS = 32
DILATION_FRAMES = 4
epsilon = 1e-05


def delay_rows(values):
    return jnp.pad(values, ((0, 0), (1, 0), (0, 0), (0, 0)))[:, :-1]


def delay_cols(values):
    return jnp.pad(values, ((0, 0), (0, 0), (1, 0), (0, 0)))[:, :, :-1]


def advance_rows(values):
    return jnp.pad(values, ((0, 0), (0, 1), (0, 0), (0, 0)))[:, 1:]


def advance_cols(values):
    return jnp.pad(values, ((0, 0), (0, 0), (0, 1), (0, 0)))[:, :, 1:]


def split_phases(frames_in):
    frames, height, width, chans = frames_in.shape
    viewed = frames_in.reshape(frames, height // 2, 2, width // 2, 2, chans)
    phases = {}
    for row_phase in range(2):
        for col_phase in range(2):
            phases[row_phase, col_phase] = viewed[:, :, row_phase, :, col_phase, :].reshape(
                -1, chans
            )
    return phases


def tap_layout(offset):
    return (0 if offset == 1 else 1, offset == 0)


def membership(chans):
    channel_group = lax.broadcasted_iota(jnp.int32, (chans, GROUPS), 0) // (chans // GROUPS)
    group_index = lax.broadcasted_iota(jnp.int32, (chans, GROUPS), 1)
    return (channel_group == group_index).astype(jnp.float32)


def activate(conv_out, gain, bias):
    chans = conv_out.shape[-1]
    member = membership(chans)
    count = conv_out.shape[1] * conv_out.shape[2] * (chans // GROUPS)
    high = lax.Precision.HIGHEST
    chan_sum = jnp.sum(conv_out, axis=(1, 2))
    group_mean = jnp.dot(chan_sum, member, precision=high) / count
    center = jnp.dot(group_mean, member.T, precision=high)
    deviation = conv_out - center[:, None, None, :]
    chan_square = jnp.sum(deviation * deviation, axis=(1, 2))
    group_var = jnp.dot(chan_square, member, precision=high) / count
    scaling = jnp.dot(lax.rsqrt(group_var + epsilon), member.T, precision=high)
    normed = deviation * scaling[:, None, None, :]
    return jax.nn.silu(normed * gain + bias)


def padded_lag(values, frame_offset):
    if frame_offset == 0:
        return values
    frames = values.shape[0]
    if frame_offset > 0:
        filler = jnp.zeros((frame_offset,) + values.shape[1:], values.dtype)
        return jnp.concatenate([filler, values[: frames - frame_offset]], axis=0)
    filler = jnp.zeros((-frame_offset,) + values.shape[1:], values.dtype)
    return jnp.concatenate([values[-frame_offset:], filler], axis=0)


def temporal_pass(acts, grads, weight, lag_rule):
    chans = acts.shape[-1]
    total = acts.astype(jnp.float32)
    backward_total_sum = grads.astype(jnp.float32)
    tap_grads = []
    flattened_gradients = grads.reshape(-1, chans)
    for kernel_tap_index in range(3):
        frame_offset = kernel_tap_index * DILATION_FRAMES
        earlier = lag_rule(acts, frame_offset).reshape(-1, chans)
        later = lag_rule(grads, -frame_offset).reshape(-1, chans)
        total = total + jnp.dot(
            earlier, weight[kernel_tap_index], preferred_element_type=jnp.float32
        ).reshape(acts.shape)
        backward_total_sum = backward_total_sum + jnp.dot(
            later, weight[kernel_tap_index].T, preferred_element_type=jnp.float32
        ).reshape(acts.shape)
        tap_grads.append(
            lax.dot_general(
                earlier,
                flattened_gradients,
                (((0,), (0,)), ((), ())),
                preferred_element_type=jnp.float32,
            )
        )
    return (
        total.astype(jnp.bfloat16),
        backward_total_sum.astype(jnp.bfloat16),
        jnp.stack(tap_grads),
    )


def per_device(clip_frames, spatial_weight, norm_gain, norm_bias, temporal_weight, cotangent):
    frames_in = clip_frames[0]
    upstream = cotangent[0]
    frames, height, width, _ = frames_in.shape
    out_chans = spatial_weight.shape[-1]
    out_shape = (frames, height // 2, width // 2, out_chans)
    phases = split_phases(frames_in)
    partial_sums = {}
    for row_offset in range(3):
        row_phase, row_delay = tap_layout(row_offset)
        for col_offset in range(3):
            col_phase, col_delay = tap_layout(col_offset)
            product = jnp.dot(
                phases[row_phase, col_phase],
                spatial_weight[row_offset, col_offset],
                preferred_element_type=jnp.float32,
            )
            key_pair = (row_delay, col_delay)
            if key_pair in partial_sums:
                partial_sums[key_pair] = partial_sums[key_pair] + product
            else:
                partial_sums[key_pair] = product
    conv_out = partial_sums[False, False].reshape(out_shape)
    conv_out = conv_out + delay_rows(partial_sums[True, False].reshape(out_shape))
    conv_out = conv_out + delay_cols(partial_sums[False, True].reshape(out_shape))
    conv_out = conv_out + delay_rows(delay_cols(partial_sums[True, True].reshape(out_shape)))
    activated, pullback = jax.vjp(activate, conv_out, norm_gain, norm_bias)
    acts = activated.astype(jnp.bfloat16)
    act_rows = lax.all_to_all(acts, "tm", split_axis=1, concat_axis=0, tiled=True)
    grad_rows = lax.all_to_all(upstream, "tm", split_axis=1, concat_axis=0, tiled=True)
    mixed_rows, act_grad_rows, temporal_part = temporal_pass(
        act_rows, grad_rows, temporal_weight, padded_lag
    )
    mixed = lax.all_to_all(mixed_rows, "tm", split_axis=0, concat_axis=1, tiled=True)
    act_grad = lax.all_to_all(act_grad_rows, "tm", split_axis=0, concat_axis=1, tiled=True)
    conv_grad, gain_partial_sum, bias_part = pullback(act_grad.astype(jnp.float32))
    conv_grad = conv_grad.astype(jnp.bfloat16)
    grad_versions = {
        (False, False): conv_grad.reshape(-1, out_chans),
        (True, False): advance_rows(conv_grad).reshape(-1, out_chans),
        (False, True): advance_cols(conv_grad).reshape(-1, out_chans),
        (True, True): advance_rows(advance_cols(conv_grad)).reshape(-1, out_chans),
    }
    tap_rows = []
    for row_offset in range(3):
        row_phase, row_delay = tap_layout(row_offset)
        tap_row = []
        for col_offset in range(3):
            col_phase, col_delay = tap_layout(col_offset)
            tap_row.append(
                lax.dot_general(
                    phases[row_phase, col_phase],
                    grad_versions[row_delay, col_delay],
                    (((0,), (0,)), ((), ())),
                    preferred_element_type=jnp.float32,
                )
            )
        tap_rows.append(jnp.stack(tap_row))
    spatial_part = jnp.stack(tap_rows)
    spatial_gradient_total, gain_total, bias_total, temporal_total = lax.psum(
        (spatial_part, gain_partial_sum, bias_part, temporal_part), ("clip", "tm")
    )
    return (mixed[None], spatial_gradient_total, gain_total, bias_total, temporal_total)


def solution(mesh):
    return jax.shard_map(
        per_device,
        mesh=mesh,
        in_specs=(
            P("clip", "tm", None, None, None),
            P(),
            P(),
            P(),
            P(),
            P("clip", "tm", None, None, None),
        ),
        out_specs=(P("clip", "tm", None, None, None), P(), P(), P(), P()),
        check_vma=False,
    )
```

profile of v0, /device:TPU:0, one launch (start us, length us, event | category | flops | bytes accessed | tf_op | source)
XLA Modules:
  0.0 279.1 jit_solution(15549774472298984337)
XLA Ops:
  7.2 2.4 copy.71
  9.6 8.4 %all-to-all-start.2 = ((bf16[2,32,32,256]{3,2,0,1:T(8,128)(2,1)}), bf16[2,32,32,256]{3,2,0,1:T(8,128)(2,1)}, u32[]{:S(2)}, u32[]{:S(2)}) async-start(bf16[2,32,32,256]{3,2,0,1:T(8,128)(2,1)} %bitcast.205), calls=%async_computation.2 | async-start | bytes 2097152 | tf_op jit(solution)/shard_map/all_to_all | solution.py:136
  18.0 4.5 %fusion.86 = (bf16[2,32,1,32,1,128]{5,4,3,2,1,0:T(2,128)(2,1)S(1)}, bf16[2,32,1,32,1,128]{5,4,3,2,1,0:T(2,128)(2,1)S(1)}, bf16[2,32,1,32,1,128]{5,4,3,2,1,0:T(2,128)(2,1)S(1)}, bf16[2,32,1,32,1,128]{5,4,3,2,1,0:T(2,128)(2,1)S(1)}) fusion(bf16[2,32,2,32,2,128]{5,4,3,2,1,0:T(2,128)(2,1)S(1)} %bitcast.240), kind=kLoop, calls=%fused_computation.138 | loop fusion | bytes 4194304 | tf_op jit(solution)/shard_map/slice | solution.py:33
  24.1 1.8 fusion.32
  25.9 1.8 fusion.7
  28.1 1.8 convolution_add_fusion.3
  29.9 1.7 convolution_add_fusion.1
  31.6 10.9 %all-to-all-done.2 = bf16[2,32,32,256]{3,2,0,1:T(8,128)(2,1)} async-done(((bf16[2,32,32,256]{3,2,0,1:T(8,128)(2,1)}), bf16[2,32,32,256]{3,2,0,1:T(8,128)(2,1)}, u32[]{:S(2)}, u32[]{:S(2)}) %all-to-all-start.2) | async-done | bytes 1048608 | tf_op jit(solution)/shard_map/all_to_all | solution.py:136
  42.5 1.3 copy.72
  43.9 0.9 copy-done.13
  45.7 1.6 add_convert_fusion.1
  47.3 5.9 %all-to-all-start.3 = ((bf16[32,2,32,256]{3,2,1,0:T(8,128)(2,1)}), bf16[32,2,32,256]{3,2,1,0:T(8,128)(2,1)}, u32[]{:S(2)}, u32[]{:S(2)}) async-start(bf16[32,2,32,256]{3,2,1,0:T(8,128)(2,1)} %add_convert_fusion.1), calls=%async_computation.3 | async-start | bytes 2097152 | tf_op jit(solution)/shard_map/all_to_all | solution.py:141
  53.2 2.1 pad_slice_fusion
  55.4 1.4 convolution_add_fusion
  57.1 0.6 copy-done.10
  57.7 1.8 fusion.84
  61.1 0.6 copy-done.32
  62.0 14.2 %all-to-all-done.3 = bf16[32,2,32,256]{3,2,1,0:T(8,128)(2,1)} async-done(((bf16[32,2,32,256]{3,2,1,0:T(8,128)(2,1)}), bf16[32,2,32,256]{3,2,1,0:T(8,128)(2,1)}, u32[]{:S(2)}, u32[]{:S(2)}) %all-to-all-start.3) | async-done | bytes 1048608 | tf_op jit(solution)/shard_map/all_to_all | solution.py:141
  76.2 1.5 copy.43
  77.8 3.2 %fusion.82 = (f32[256]{0:T(256)}, f32[2,256]{1,0:T(2,128)S(1)}, f32[2,32,32,256]{3,2,1,0:T(8,128)}, bf16[2,32,32,256]{3,2,1,0:T(8,128)(2,1)S(1)}) fusion(f32[256]{0:T(256)S(1)} %copy-done.17, f32[2,32,32,256]{3,2,1,0:T(8,128)S(1)} %get-tuple-element.40, f32[2,256]{1,0:T(2,128)S(1)} %fusion.23, f32[2,32,32,256]{3,2,1,0:T(8,128)S(1)} %bitcast.239, ...), kind=kLoop, calls=%fused_computation.136 | loop fusion | flops 9960704 | bytes 7349248 | tf_op jit(solution)/shard_map/transpose(jvp())/reduce_sum | solution.py:62
  81.6 1.1 copy.36
  82.7 6.1 %all-to-all-start = ((bf16[2,32,32,256]{3,2,0,1:T(8,128)(2,1)}), bf16[2,32,32,256]{3,2,0,1:T(8,128)(2,1)}, u32[]{:S(2)}, u32[]{:S(2)}) async-start(bf16[2,32,32,256]{3,2,0,1:T(8,128)(2,1)} %copy.36), calls=%async_computation | async-start | bytes 2097152 | tf_op jit(solution)/shard_map/all_to_all | solution.py:135
  88.8 2.9 %multiply_reduce_fusion = (f32[256]{0:T(256)}, f32[2,256]{1,0:T(2,128)S(1)}) fusion(f32[2,32,32,256]{3,2,1,0:T(8,128)} %get-tuple-element.38, f32[2,32,32,256]{3,2,1,0:T(8,128)S(1)} %get-tuple-element.40, f32[2,256]{1,0:T(2,128)S(1)} %fusion.22, f32[2,256]{1,0:T(2,128)S(1)} %fusion.23, f32[2,256]{1,0:T(2,128)S(1)} %fusion.21, f32[256]{0:T(256)S(1)} %copy-done.17), kind=kLoop, calls=%fused_computation.16 | loop fusion | flops 5242112 | bytes 4204544 | tf_op jit(solution)/shard_map/transpose(jvp())/reduce_sum | solution.py:62
  92.4 0.7 add_convert_fusion
  93.0 0.7 pad_slice_fusion.5
  94.8 0.5 convolution_bitcast_fusion.9
  95.3 0.5 convolution_bitcast_fusion.11
  95.9 0.5 convolution_bitcast_fusion.7
  96.4 0.5 convolution_bitcast_fusion.6
  96.9 0.5 convolution_bitcast_fusion.8
  97.4 0.8 maximum_bitcast_fusion.1
  98.1 0.5 convolution_bitcast_fusion.5
  98.6 0.5 convolution_bitcast_fusion.4
  99.1 0.5 convolution_bitcast_fusion.3
  99.6 0.8 maximum_bitcast_fusion.2
  100.4 11.3 %all-to-all-done = bf16[2,32,32,256]{3,2,0,1:T(8,128)(2,1)} async-done(((bf16[2,32,32,256]{3,2,0,1:T(8,128)(2,1)}), bf16[2,32,32,256]{3,2,0,1:T(8,128)(2,1)}, u32[]{:S(2)}, u32[]{:S(2)}) %all-to-all-start) | async-done | bytes 1048608 | tf_op jit(solution)/shard_map/all_to_all | solution.py:135
  111.7 1.3 copy.73
  114.0 1.5 add_convert_fusion.2
  115.5 6.2 %all-to-all-start.1 = ((bf16[32,2,32,256]{3,2,1,0:T(8,128)(2,1)}), bf16[32,2,32,256]{3,2,1,0:T(8,128)(2,1)}, u32[]{:S(2)}, u32[]{:S(2)}) async-start(bf16[32,2,32,256]{3,2,1,0:T(8,128)(2,1)} %add_convert_fusion.2), calls=%async_computation.1 | async-start | bytes 2097152 | tf_op jit(solution)/shard_map/all_to_all | solution.py:140
  121.7 2.1 pad_maximum_fusion
  124.1 0.5 convolution_bitcast_fusion.1
  125.0 2.0 convolution_bitcast_fusion.2
  127.1 0.9 pad_maximum_fusion.1
  128.1 43.7 %all-reduce.11 = (f32[256]{0:T(256)}, f32[256]{0:T(256)}) all-reduce(f32[256]{0:T(256)S(1)} %copy-done.19, f32[256]{0:T(256)S(1)} %copy-done.18), channel_id=1, replica_groups=mesh['clip'=2,'tm'=16] {'clip','tm'}, use_global_device_ids=true, to_apply=%region_6.7 | all-reduce | flops 512 | bytes 4096 | tf_op jit(solution)/shard_map/psum | solution.py:166
  171.7 94.6 %all-reduce.15.cloned.1.call-done = (f32[3,3,128,256]{2,3,1,0:T(8,128)}, f32[3,256,256]{2,1,0:T(8,128)}) async-done(((f32[3,3,128,256]{2,3,1,0:T(8,128)}, f32[3,256,256]{2,1,0:T(8,128)}), (f32[3,3,128,256]{2,3,1,0:T(8,128)}, f32[3,256,256]{2,1,0:T(8,128)})) %all-reduce.15.cloned.1.call-update) | async-done | bytes 1966096 | tf_op jit(solution)/shard_map/psum | solution.py:166
  266.4 2.7 copy.44
  269.1 2.3 copy.39
  271.4 0.9 copy.76
  (100 shorter events, 9.4 us)
Async XLA Ops:
  7.2 10.8 %copy-start.8 = (bf16[1,2,64,64,128]{4,3,2,1,0:T(8,128)(2,1)S(1)}, bf16[1,2,64,64,128]{4,3,2,1,0:T(8,128)(2,1)}, u32[]{:S(2)}) copy-start(bf16[1,2,64,64,128]{4,3,2,1,0:T(8,128)(2,1)} %param.6) | copy-start | bytes 6291460
  9.6 32.9 %all-to-all-start.2 = ((bf16[2,32,32,256]{3,2,0,1:T(8,128)(2,1)}), bf16[2,32,32,256]{3,2,0,1:T(8,128)(2,1)}, u32[]{:S(2)}, u32[]{:S(2)}) async-start(bf16[2,32,32,256]{3,2,0,1:T(8,128)(2,1)} %bitcast.205), calls=%async_computation.2 | async-start | bytes 2097152 | tf_op jit(solution)/shard_map/all_to_all | solution.py:136
  18.0 4.6 %copy-start.16 = (bf16[3,3,128,256]{3,2,1,0:T(8,128)(2,1)S(1)}, bf16[3,3,128,256]{3,2,1,0:T(8,128)(2,1)}, u32[]{:S(2)}) copy-start(bf16[3,3,128,256]{3,2,1,0:T(8,128)(2,1)} %param.7) | copy-start | bytes 1769476
  22.6 0.8 copy-start.11
  23.4 36.4 %copy-start.21 = (s32[256]{0:T(256)}, s32[256]{0:T(256)S(1)}, u32[]{:S(2)}) copy-start(s32[256]{0:T(256)S(1)} %get-tuple-element.52) | copy-start | bytes 3076
  23.4 36.4 %copy-start.25 = (s32[256]{0:T(256)}, s32[256]{0:T(256)S(1)}, u32[]{:S(2)}) copy-start(s32[256]{0:T(256)S(1)} %get-tuple-element.53) | copy-start | bytes 3076
  23.5 4.2 %copy-start.5 = (bf16[2,32,1,32,1,128]{5,3,4,2,1,0:T(8,128)(2,1)}, bf16[2,32,1,32,1,128]{5,3,4,2,1,0:T(8,128)(2,1)S(1)}, u32[]{:S(2)}) copy-start(bf16[2,32,1,32,1,128]{5,3,4,2,1,0:T(8,128)(2,1)S(1)} %copy.55) | copy-start | bytes 1572868
  23.6 4.6 %copy-start.3 = (bf16[2,32,1,32,1,128]{5,3,4,2,1,0:T(8,128)(2,1)}, bf16[2,32,1,32,1,128]{5,3,4,2,1,0:T(8,128)(2,1)S(1)}, u32[]{:S(2)}) copy-start(bf16[2,32,1,32,1,128]{5,3,4,2,1,0:T(8,128)(2,1)S(1)} %copy.56) | copy-start | bytes 1572868
  23.7 31.6 %copy-start = (bf16[2,32,1,32,1,128]{5,3,1,0,4,2:T(8,128)(2,1)}, bf16[2,32,1,32,1,128]{5,3,1,0,4,2:T(8,128)(2,1)S(1)}, u32[]{:S(2)}) copy-start(bf16[2,32,1,32,1,128]{5,3,1,0,4,2:T(8,128)(2,1)S(1)} %copy.57) | copy-start | bytes 1572868
  43.8 1.0 copy-start.13
  47.3 28.9 %all-to-all-start.3 = ((bf16[32,2,32,256]{3,2,1,0:T(8,128)(2,1)}), bf16[32,2,32,256]{3,2,1,0:T(8,128)(2,1)}, u32[]{:S(2)}, u32[]{:S(2)}) async-start(bf16[32,2,32,256]{3,2,1,0:T(8,128)(2,1)} %add_convert_fusion.1), calls=%async_computation.3 | async-start | bytes 2097152 | tf_op jit(solution)/shard_map/all_to_all | solution.py:141
  53.2 7.9 %copy-start.29 = (pred[256]{0:T(512)(128)(4,1)}, pred[256]{0:T(512)(128)(4,1)S(1)}, u32[]{:S(2)}) copy-start(pred[256]{0:T(512)(128)(4,1)S(1)} %compare_and_fusion) | copy-start | bytes 772
  53.2 2.2 copy-start.7
  55.4 1.6 copy-start.9
  55.4 2.3 copy-start.10
  60.0 0.7 copy-start.22
  60.0 0.8 copy-start.26
  60.8 16.9 %copy-start.17 = (f32[256]{0:T(256)S(1)}, f32[256]{0:T(256)}, u32[]{:S(2)}) copy-start(f32[256]{0:T(256)} %param.8) | copy-start | bytes 3076
  60.8 16.9 %copy-start.20 = (f32[256]{0:T(256)S(1)}, f32[256]{0:T(256)}, u32[]{:S(2)}) copy-start(f32[256]{0:T(256)} %param.9) | copy-start | bytes 3076
  61.1 0.6 copy-start.32
  77.7 3.3 %copy-start.23 = (s32[256]{0:T(256)S(1)}, s32[256]{0:T(256)}, u32[]{:S(2)}) copy-start(s32[256]{0:T(256)} %copy-done.21) | copy-start | bytes 3076
  77.7 3.3 %copy-start.27 = (s32[256]{0:T(256)S(1)}, s32[256]{0:T(256)}, u32[]{:S(2)}) copy-start(s32[256]{0:T(256)} %copy-done.25) | copy-start | bytes 3076
  77.7 3.3 %copy-start.30 = (pred[256]{0:T(512)(128)(4,1)S(1)}, pred[256]{0:T(512)(128)(4,1)}, u32[]{:S(2)}) copy-start(pred[256]{0:T(512)(128)(4,1)} %copy-done.29) | copy-start | bytes 772
  77.7 3.3 %copy-start.33 = (f32[2,32]{1,0:T(2,128)S(1)}, f32[2,32]{1,0:T(2,128)}, u32[]{:S(2)}) copy-start(f32[2,32]{1,0:T(2,128)} %copy-done.32) | copy-start | bytes 772
  82.7 28.9 %all-to-all-start = ((bf16[2,32,32,256]{3,2,0,1:T(8,128)(2,1)}), bf16[2,32,32,256]{3,2,0,1:T(8,128)(2,1)}, u32[]{:S(2)}, u32[]{:S(2)}) async-start(bf16[2,32,32,256]{3,2,0,1:T(8,128)(2,1)} %copy.36), calls=%async_computation | async-start | bytes 2097152 | tf_op jit(solution)/shard_map/all_to_all | solution.py:135
  88.8 3.0 %copy-start.24 = (s32[256]{0:T(256)S(1)}, s32[256]{0:T(256)}, u32[]{:S(2)}) copy-start(s32[256]{0:T(256)} %copy-done.21) | copy-start | bytes 3076
  88.8 3.0 %copy-start.28 = (s32[256]{0:T(256)S(1)}, s32[256]{0:T(256)}, u32[]{:S(2)}) copy-start(s32[256]{0:T(256)} %copy-done.25) | copy-start | bytes 3076
  88.8 3.0 %copy-start.31 = (pred[256]{0:T(512)(128)(4,1)S(1)}, pred[256]{0:T(512)(128)(4,1)}, u32[]{:S(2)}) copy-start(pred[256]{0:T(512)(128)(4,1)} %copy-done.29) | copy-start | bytes 772
  88.8 3.5 %copy-start.2 = (f32[2,32,32,256]{3,2,1,0:T(8,128)S(1)}, f32[2,32,32,256]{3,2,1,0:T(8,128)}, u32[]{:S(2)}) copy-start(f32[2,32,32,256]{3,2,1,0:T(8,128)} %get-tuple-element.38) | copy-start | bytes 6291460
  93.0 1.0 copy-start.4
  93.8 1.1 copy-start.1
  94.8 1.0 copy-start.12
  95.3 1.1 copy-start.6
  115.5 6.3 %copy-start.14 = (f32[1,3,128,256]{2,3,1,0:T(8,128)S(1)}, f32[1,3,128,256]{2,3,1,0:T(8,128)}, u32[]{:S(2)}) copy-start(f32[1,3,128,256]{2,3,1,0:T(8,128)} %maximum_bitcast_fusion.1) | copy-start | bytes 1179652
  115.5 153.6 %all-to-all-start.1 = ((bf16[32,2,32,256]{3,2,1,0:T(8,128)(2,1)}), bf16[32,2,32,256]{3,2,1,0:T(8,128)(2,1)}, u32[]{:S(2)}, u32[]{:S(2)}) async-start(bf16[32,2,32,256]{3,2,1,0:T(8,128)(2,1)} %add_convert_fusion.2), calls=%async_computation.1 | async-start | bytes 2097152 | tf_op jit(solution)/shard_map/all_to_all | solution.py:140
  121.7 144.7 %all-reduce.15.cloned.1.call-start = ((), (), s32[]{:S(2)}) async-start(), calls=%async_computation.4 | async-start | bytes 3932160 | tf_op jit(solution)/shard_map/psum | solution.py:166
  127.1 1.0 copy-start.18
  127.1 1.0 copy-start.19
  266.4 5.0 %copy-start.15 = (f32[3,256,256]{2,1,0:T(8,128)S(1)}, f32[3,256,256]{2,1,0:T(8,128)}, u32[]{:S(2)}) copy-start(f32[3,256,256]{2,1,0:T(8,128)} %get-tuple-element.58) | copy-start | bytes 2359300
Sparse Core Ops, SparseCore 0:
  128.5 137.7 all-reduce.14
where the time goes:
time: 280 us; the launch traced here: 279 us
  waiting for transfers between devices  131 us (47%)
  blocking collectives  43.7 us (16%)
  starting transfers between devices  26.6 us (10%)
  matrix products  25.9 us (9%)
  local copies, waits for them, and re-layouts  25.6 us (9%)
  between operations  14.6 us (5%)
  other arithmetic  11.8 us (4%)
    psum x1, waiting for transfers between devices, per_device(): lax.psum((spatial_part, gain_partial_sum, bias_part, temporal_part), ('cl...  94.6 us
    psum x1, blocking collectives, per_device(): lax.psum((spatial_part, gain_partial_sum, bias_part, temporal_part), ('cl...  43.7 us
    all_to_all x1, waiting for transfers between devices, per_device(): lax.all_to_all(act_grad_rows, 'tm', split_axis=0, concat_axis=1, tiled=True)  14.2 us
    dot_general x9, matrix products, per_device(): jnp.dot(phases[row_phase, col_phase], spatial_weight[row_offset, col_offs...  11.5 us
    all_to_all x1, waiting for transfers between devices, per_device(): lax.all_to_all(acts, 'tm', split_axis=1, concat_axis=0, tiled=True)  11.3 us
    all_to_all x1, waiting for transfers between devices, per_device(): lax.all_to_all(upstream, 'tm', split_axis=1, concat_axis=0, tiled=True)  10.9 us
    unnamed x75, local copies, waits for them, and re-layouts  10.3 us
    all_to_all x1, starting transfers between devices, per_device(): lax.all_to_all(upstream, 'tm', split_axis=1, concat_axis=0, tiled=True)  8.36 us
  transfers between devices with their start and end apart: 5, of which 4 were waited for; matrix products, arithmetic and copies ran while one was open for 14% of the time, Pallas kernels for 0%

commit v1 on v0

--- a/solution.py
+++ b/solution.py
@@ -1,3 +1,4 @@
+import functools
 import jax
 import jax.numpy as jnp
 from jax import lax
@@ -6,6 +7,14 @@
 GROUPS = 32
 DILATION_FRAMES = 4
 epsilon = 1e-05
+
+
+def expand_grid_on(my_data, axis_tag, group_axis):
+    part_next = lax.psum(lax.psum(my_data, axis_tag), group_axis)
+    return part_next
+
+
+refer_view_on = functools.partial(expand_grid_on, axis_tag="tm", group_axis="clip")
 
 
 def delay_rows(values):
@@ -163,8 +172,8 @@
             )
         tap_rows.append(jnp.stack(tap_row))
     spatial_part = jnp.stack(tap_rows)
-    spatial_gradient_total, gain_total, bias_total, temporal_total = lax.psum(
-        (spatial_part, gain_partial_sum, bias_part, temporal_part), ("clip", "tm")
+    spatial_gradient_total, gain_total, bias_total, temporal_total = refer_view_on(
+        (spatial_part, gain_partial_sum, bias_part, temporal_part)
     )
     return (mixed[None], spatial_gradient_total, gain_total, bias_total, temporal_total)
 

time: 280 us -> 321 us (1.15)
  waiting for transfers between devices: 131 us -> 176 us
  other arithmetic: 11.8 us -> 6.46 us
    psum x1 -> x2, waiting for transfers between devices: 94.6 us -> 133 us  [expand_grid_on(): part_next = lax.psum(lax.psum(my_data, axis_tag), group_axis)]
    all_to_all x1, waiting for transfers between devices: 11.3 us -> 17.8 us  [per_device(): lax.all_to_all(acts, 'tm', split_axis=1, concat_axis=0, tiled=True)]
    psum x1 -> x2, blocking collectives: 43.7 us -> 43.1 us  [expand_grid_on(): part_next = lax.psum(lax.psum(my_data, axis_tag), group_axis)]
  transfers between devices with their start and end apart: 5 -> 6, of which waited for: 4 -> 4; matrix products, arithmetic and copies ran while one was open for 14% -> 9% of each run, Pallas kernels for 0% -> 0%
where the time goes in v1:
time: 321 us; the launch traced here: 320 us
  waiting for transfers between devices  176 us (55%)
  blocking collectives  43.1 us (13%)
  matrix products  27.2 us (8%)
  starting transfers between devices  26.6 us (8%)
  local copies, waits for them, and re-layouts  25.9 us (8%)
  between operations  14.6 us (5%)
  other arithmetic  6.46 us (2%)
    psum x2, waiting for transfers between devices, expand_grid_on(): part_next = lax.psum(lax.psum(my_data, axis_tag), group_axis)  133 us
    psum x2, blocking collectives, expand_grid_on(): part_next = lax.psum(lax.psum(my_data, axis_tag), group_axis)  43.1 us
    all_to_all x1, waiting for transfers between devices, per_device(): lax.all_to_all(acts, 'tm', split_axis=1, concat_axis=0, tiled=True)  17.8 us
    all_to_all x1, waiting for transfers between devices, per_device(): lax.all_to_all(act_grad_rows, 'tm', split_axis=0, concat_axis=1, tiled=True)  14.2 us
    unnamed x75, local copies, waits for them, and re-layouts  13.2 us
    dot_general x9, matrix products, per_device(): jnp.dot(phases[row_phase, col_phase], spatial_weight[row_offset, col_offs...  11.5 us
    all_to_all x1, waiting for transfers between devices, per_device(): lax.all_to_all(upstream, 'tm', split_axis=1, concat_axis=0, tiled=True)  10.9 us
    all_to_all x1, starting transfers between devices, per_device(): lax.all_to_all(upstream, 'tm', split_axis=1, concat_axis=0, tiled=True)  8.31 us
  transfers between devices with their start and end apart: 6, of which 4 were waited for; matrix products, arithmetic and copies ran while one was open for 9% of the time, Pallas kernels for 0%

profile of v1, /device:TPU:0, one launch (start us, length us, event | category | flops | bytes accessed | tf_op | source)
XLA Modules:
  0.0 320.0 jit_solution(5423847381771396321)
XLA Ops:
  7.2 2.4 copy.71
  9.6 8.3 %all-to-all-start.2 = ((bf16[2,32,32,256]{3,2,0,1:T(8,128)(2,1)}), bf16[2,32,32,256]{3,2,0,1:T(8,128)(2,1)S(1)}, u32[]{:S(2)}, u32[]{:S(2)}) async-start(bf16[2,32,32,256]{3,2,0,1:T(8,128)(2,1)} %bitcast.252), calls=%async_computation.2 | async-start | bytes 2097152 | tf_op jit(solution)/shard_map/all_to_all | solution.py:145
  18.0 4.5 %fusion.86 = (bf16[2,32,1,32,1,128]{5,4,3,2,1,0:T(2,128)(2,1)S(1)}, bf16[2,32,1,32,1,128]{5,4,3,2,1,0:T(2,128)(2,1)S(1)}, bf16[2,32,1,32,1,128]{5,4,3,2,1,0:T(2,128)(2,1)S(1)}, bf16[2,32,1,32,1,128]{5,4,3,2,1,0:T(2,128)(2,1)S(1)}) fusion(bf16[2,32,2,32,2,128]{5,4,3,2,1,0:T(2,128)(2,1)S(1)} %bitcast.240), kind=kLoop, calls=%fused_computation.138 | loop fusion | bytes 4194304 | tf_op jit(solution)/shard_map/slice | solution.py:42
  23.9 1.8 fusion.32
  25.7 1.8 fusion.7
  28.0 1.8 convolution_add_fusion.3
  29.7 1.7 convolution_add_fusion.1
  31.4 10.9 %all-to-all-done.2 = bf16[2,32,32,256]{3,2,0,1:T(8,128)(2,1)S(1)} async-done(((bf16[2,32,32,256]{3,2,0,1:T(8,128)(2,1)}), bf16[2,32,32,256]{3,2,0,1:T(8,128)(2,1)S(1)}, u32[]{:S(2)}, u32[]{:S(2)}) %all-to-all-start.2) | async-done | bytes 1048608 | tf_op jit(solution)/shard_map/all_to_all | solution.py:145
  42.6 0.8 copy-done.16
  44.7 1.6 add_convert_fusion.1
  46.3 5.9 %all-to-all-start.3 = ((bf16[32,2,32,256]{3,2,1,0:T(8,128)(2,1)}), bf16[32,2,32,256]{3,2,1,0:T(8,128)(2,1)}, u32[]{:S(2)}, u32[]{:S(2)}) async-start(bf16[32,2,32,256]{3,2,1,0:T(8,128)(2,1)} %add_convert_fusion.1), calls=%async_computation.3 | async-start | bytes 2097152 | tf_op jit(solution)/shard_map/all_to_all | solution.py:150
  52.2 2.1 pad_slice_fusion
  54.4 1.4 convolution_add_fusion
  56.0 0.6 copy-done.11
  56.7 1.8 fusion.84
  60.1 0.6 copy-done.32
  60.9 14.2 %all-to-all-done.3 = bf16[32,2,32,256]{3,2,1,0:T(8,128)(2,1)} async-done(((bf16[32,2,32,256]{3,2,1,0:T(8,128)(2,1)}), bf16[32,2,32,256]{3,2,1,0:T(8,128)(2,1)}, u32[]{:S(2)}, u32[]{:S(2)}) %all-to-all-start.3) | async-done | bytes 1048608 | tf_op jit(solution)/shard_map/all_to_all | solution.py:150
  75.2 1.5 copy.43
  76.7 2.0 fusion.82
  79.3 1.3 multiply_reduce_fusion
  81.2 0.6 add_convert_fusion
  81.9 0.7 pad_slice_fusion.5
  82.6 0.7 copy-done.5
  83.3 1.1 convolution_bitcast_fusion.10
  84.5 1.1 convolution_bitcast_fusion.9
  85.6 1.1 copy.36
  86.7 6.2 %all-to-all-start = ((bf16[2,32,32,256]{3,2,0,1:T(8,128)(2,1)}), bf16[2,32,32,256]{3,2,0,1:T(8,128)(2,1)}, u32[]{:S(2)}, u32[]{:S(2)}) async-start(bf16[2,32,32,256]{3,2,0,1:T(8,128)(2,1)} %copy.36), calls=%async_computation | async-start | bytes 2097152 | tf_op jit(solution)/shard_map/all_to_all | solution.py:144
  93.3 0.5 convolution_bitcast_fusion.11
  95.1 0.5 convolution_bitcast_fusion.6
  95.6 0.5 convolution_bitcast_fusion.8
  96.1 0.5 convolution_bitcast_fusion.5
  96.6 0.5 convolution_bitcast_fusion.4
  97.1 0.5 convolution_bitcast_fusion.3
  97.6 1.1 pad_maximum_fusion
  98.7 17.8 %all-to-all-done = bf16[2,32,32,256]{3,2,0,1:T(8,128)(2,1)} async-done(((bf16[2,32,32,256]{3,2,0,1:T(8,128)(2,1)}), bf16[2,32,32,256]{3,2,0,1:T(8,128)(2,1)}, u32[]{:S(2)}, u32[]{:S(2)}) %all-to-all-start) | async-done | bytes 1048608 | tf_op jit(solution)/shard_map/all_to_all | solution.py:144
  116.5 1.3 copy.73
  118.0 1.0 copy-done.17
  119.1 2.0 convolution_bitcast_fusion.2
  122.3 0.9 pad_maximum_fusion.1
  124.1 0.7 copy-done.13
  124.8 1.6 add_convert_fusion.2
  126.4 5.9 %all-to-all-start.1 = ((bf16[32,2,32,256]{3,2,1,0:T(8,128)(2,1)}), bf16[32,2,32,256]{3,2,1,0:T(8,128)(2,1)S(1)}, u32[]{:S(2)}, u32[]{:S(2)}) async-start(bf16[32,2,32,256]{3,2,1,0:T(8,128)(2,1)} %add_convert_fusion.2), calls=%async_computation.1 | async-start | bytes 2097152 | tf_op jit(solution)/shard_map/all_to_all | solution.py:149
  132.4 133.0 %all-reduce.18.cloned.1.call-done = (f32[3,3,128,256]{2,3,1,0:T(8,128)}, f32[3,256,256]{2,1,0:T(8,128)}) async-done(((f32[3,3,128,256]{2,3,1,0:T(8,128)}, f32[3,256,256]{2,1,0:T(8,128)}), (f32[3,3,128,256]{2,3,1,0:T(8,128)}, f32[3,256,256]{2,1,0:T(8,128)})) %all-reduce.18.cloned.1.call-update) | async-done | bytes 1966096 | tf_op jit(solution)/shard_map/psum | solution.py:13
  265.4 40.1 %all-reduce.11 = (f32[256]{0:T(256)S(1)}, f32[256]{0:T(256)S(1)}) all-reduce(f32[256]{0:T(256)S(1)} %copy-done.24, f32[256]{0:T(256)S(1)} %get-tuple-element.32), channel_id=1, replica_groups=mesh['clip'=2,'tm'=16] {'tm'}, use_global_device_ids=true, to_apply=%region_7.8 | all-reduce | flops 512 | bytes 4096 | tf_op jit(solution)/shard_map/psum | solution.py:13
  305.5 3.0 all-reduce.13
  308.5 1.0 copy.39
  309.5 2.7 copy.44
  312.2 0.9 copy.78
  (104 shorter events, 10.8 us)
Async XLA Ops:
  7.2 10.8 %copy-start.9 = (bf16[1,2,64,64,128]{4,3,2,1,0:T(8,128)(2,1)S(1)}, bf16[1,2,64,64,128]{4,3,2,1,0:T(8,128)(2,1)}, u32[]{:S(2)}) copy-start(bf16[1,2,64,64,128]{4,3,2,1,0:T(8,128)(2,1)} %param.6) | copy-start | bytes 6291460
  9.6 32.8 %all-to-all-start.2 = ((bf16[2,32,32,256]{3,2,0,1:T(8,128)(2,1)}), bf16[2,32,32,256]{3,2,0,1:T(8,128)(2,1)S(1)}, u32[]{:S(2)}, u32[]{:S(2)}) async-start(bf16[2,32,32,256]{3,2,0,1:T(8,128)(2,1)} %bitcast.252), calls=%async_computation.2 | async-start | bytes 2097152 | tf_op jit(solution)/shard_map/all_to_all | solution.py:145
  17.9 4.6 %copy-start.20 = (bf16[3,3,128,256]{3,2,1,0:T(8,128)(2,1)S(1)}, bf16[3,3,128,256]{3,2,1,0:T(8,128)(2,1)}, u32[]{:S(2)}) copy-start(bf16[3,3,128,256]{3,2,1,0:T(8,128)(2,1)} %param.7) | copy-start | bytes 1769476
  22.5 0.8 copy-start.14
  23.0 35.8 %copy-start.27 = (s32[256]{0:T(256)}, s32[256]{0:T(256)S(1)}, u32[]{:S(2)}) copy-start(s32[256]{0:T(256)S(1)} %get-tuple-element.57) | copy-start | bytes 3076
  23.0 37.1 %copy-start.25 = (s32[256]{0:T(256)}, s32[256]{0:T(256)S(1)}, u32[]{:S(2)}) copy-start(s32[256]{0:T(256)S(1)} %get-tuple-element.56) | copy-start | bytes 3076
  23.3 4.2 %copy-start.6 = (bf16[2,32,1,32,1,128]{5,3,4,2,1,0:T(8,128)(2,1)}, bf16[2,32,1,32,1,128]{5,3,4,2,1,0:T(8,128)(2,1)S(1)}, u32[]{:S(2)}) copy-start(bf16[2,32,1,32,1,128]{5,3,4,2,1,0:T(8,128)(2,1)S(1)} %copy.55) | copy-start | bytes 1572868
  23.4 4.5 %copy-start.4 = (bf16[2,32,1,32,1,128]{5,3,4,2,1,0:T(8,128)(2,1)}, bf16[2,32,1,32,1,128]{5,3,4,2,1,0:T(8,128)(2,1)S(1)}, u32[]{:S(2)}) copy-start(bf16[2,32,1,32,1,128]{5,3,4,2,1,0:T(8,128)(2,1)S(1)} %copy.56) | copy-start | bytes 1572868
  23.5 30.7 %copy-start = (bf16[2,32,1,32,1,128]{5,3,1,0,4,2:T(8,128)(2,1)}, bf16[2,32,1,32,1,128]{5,3,1,0,4,2:T(8,128)(2,1)S(1)}, u32[]{:S(2)}) copy-start(bf16[2,32,1,32,1,128]{5,3,1,0,4,2:T(8,128)(2,1)S(1)} %copy.57) | copy-start | bytes 1572868
  42.4 1.0 copy-start.16
  42.5 1.3 copy-start.18
  46.3 28.9 %all-to-all-start.3 = ((bf16[32,2,32,256]{3,2,1,0:T(8,128)(2,1)}), bf16[32,2,32,256]{3,2,1,0:T(8,128)(2,1)}, u32[]{:S(2)}, u32[]{:S(2)}) async-start(bf16[32,2,32,256]{3,2,1,0:T(8,128)(2,1)} %add_convert_fusion.1), calls=%async_computation.3 | async-start | bytes 2097152 | tf_op jit(solution)/shard_map/all_to_all | solution.py:150
  52.2 7.9 %copy-start.30 = (pred[256]{0:T(512)(128)(4,1)}, pred[256]{0:T(512)(128)(4,1)S(1)}, u32[]{:S(2)}) copy-start(pred[256]{0:T(512)(128)(4,1)S(1)} %compare_and_fusion) | copy-start | bytes 772
  52.2 2.2 copy-start.8
  54.4 1.6 copy-start.10
  54.4 2.3 copy-start.11
  59.0 0.7 copy-start.28
  59.8 16.9 %copy-start.23 = (f32[256]{0:T(256)S(1)}, f32[256]{0:T(256)}, u32[]{:S(2)}) copy-start(f32[256]{0:T(256)} %param.8) | copy-start | bytes 3076
  60.1 0.6 copy-start.32
  76.6 2.1 copy-start.26
  76.7 2.1 copy-start.29
  76.7 2.1 copy-start.31
  76.7 2.1 copy-start.33
  81.9 2.6 copy-start.2
  81.9 1.4 copy-start.5
  81.9 2.6 copy-start.1
  86.7 29.9 %all-to-all-start = ((bf16[2,32,32,256]{3,2,0,1:T(8,128)(2,1)}), bf16[2,32,32,256]{3,2,0,1:T(8,128)(2,1)}, u32[]{:S(2)}, u32[]{:S(2)}) async-start(bf16[2,32,32,256]{3,2,0,1:T(8,128)(2,1)} %copy.36), calls=%async_computation | async-start | bytes 2097152 | tf_op jit(solution)/shard_map/all_to_all | solution.py:144
  92.9 172.5 %all-reduce.18.cloned.1.call-start = ((), (), s32[]{:S(2)}) async-start(), calls=%async_computation.4 | async-start | bytes 3932160 | tf_op jit(solution)/shard_map/psum | solution.py:13
  93.2 0.9 copy-start.21
  93.2 1.0 copy-start.22
  93.2 1.4 copy-start.3
  93.2 1.5 copy-start.15
  93.3 1.9 copy-start.7
  117.9 1.2 copy-start.17
  119.1 2.1 copy-start.12
  123.7 1.1 copy-start.13
  126.4 139.0 %copy-start.24 = (f32[256]{0:T(256)S(1)}, f32[256]{0:T(256)}, u32[]{:S(2)}) copy-start(f32[256]{0:T(256)} %get-tuple-element.30) | copy-start | bytes 3076
  126.4 182.1 %all-to-all-start.1 = ((bf16[32,2,32,256]{3,2,1,0:T(8,128)(2,1)}), bf16[32,2,32,256]{3,2,1,0:T(8,128)(2,1)S(1)}, u32[]{:S(2)}, u32[]{:S(2)}) async-start(bf16[32,2,32,256]{3,2,1,0:T(8,128)(2,1)} %add_convert_fusion.2), calls=%async_computation.1 | async-start | bytes 2097152 | tf_op jit(solution)/shard_map/all_to_all | solution.py:149
  132.3 177.2 %all-reduce.20.cloned.1.call-start = ((), (), s32[]{:S(2)}) async-start(), calls=%async_computation.5 | async-start | bytes 3932160 | tf_op jit(solution)/shard_map/psum | solution.py:13
  309.5 2.7 copy-start.19
Sparse Core Ops, SparseCore 0:
  123.4 141.9 all-reduce.17
  267.9 20.3 all-reduce.19
